TPU v7x, 32 devices: a whole 2x2x4 slice. The times are simulated.
32 devices in a mesh: rows: 4 (over x, core), cols: 8 (over z, y).
Axes of the slice: x: 2, y: 2, z: 4, core: 2. Of those that a mesh axis runs over, the one named last changes fastest.
Arguments:
- image: bfloat16 [48, 64, 2048], P(None, 'rows', 'cols'), may hold values from -6 to 6
- perturb: float32 [48, 64, 2048], P(None, 'rows', 'cols'), may hold values from -0.5 to 0.5
- target: bfloat16 [48, 32, 1024], P(None, 'rows', 'cols'), may hold values from -6 to 6
- kernel_one: float32 [48, 48, 3, 3], replicated, may hold values from -0.3125 to 0.3125
- kernel_two: float32 [48, 48, 3, 3], replicated, may hold values from -0.3125 to 0.3125
- moment_one: float32 [48, 48, 3, 3], replicated, may hold values from -6 to 6
- moment_two: float32 [48, 48, 3, 3], replicated, may hold values from -6 to 6
Outputs:
- new_perturb: float32 [48, 64, 2048], P(None, 'rows', 'cols')
- prediction: bfloat16 [48, 32, 1024], P(None, 'rows', 'cols')
- new_kernel_one: float32 [48, 48, 3, 3], replicated
- new_kernel_two: float32 [48, 48, 3, 3], replicated
- new_moment_one: float32 [48, 48, 3, 3], replicated
- new_moment_two: float32 [48, 48, 3, 3], replicated
All inputs are finite; a program needn't handle non-finite values.
Results may differ from a plain program's by a relative error of at most 0.0085.
Values may be sent and summed in bfloat16 or wider, within the bound.
A program may use at most 128 MiB of HBM per device.

v0:
```python
import jax
import jax.numpy as jnp
from jax import lax
from jax.sharding import PartitionSpec as P

REPLAYS = 3
step_size = 0.5
clip_bound = 0.5
momentum_rate = 0.9
learn_rate = 0.005
mean_epsilon = 1e-06
numbers = ("NCHW", "OIHW", "NCHW")


def with_halo(block, sides, width):
    for axis, dim in sides:
        count = lax.axis_size(axis)
        forward = [(i, i + 1) for i in range(count - 1)]
        backward = [(target, source) for source, target in forward]
        low = lax.ppermute(
            lax.slice_in_dim(block, block.shape[dim] - width, None, axis=dim), axis, forward
        )
        high = lax.ppermute(lax.slice_in_dim(block, 0, width, axis=dim), axis, backward)
        block = jnp.concatenate([low, block, high], axis=dim)
    return block


def shifted(block, axis, distance):
    devices = range(lax.axis_size(axis))
    route = [(i - distance, i) for i in devices if i - distance in devices]
    return lax.ppermute(block, axis, route)


def plain_conv(source, kernel, stride, dilation):
    return lax.conv_general_dilated(
        source[None],
        kernel,
        (stride, stride),
        "VALID",
        rhs_dilation=(dilation, dilation),
        dimension_numbers=numbers,
        preferred_element_type=jnp.float32,
    )[0]


def kernel_grad(source, grad_out, stride, dilation):
    summed = lax.conv_general_dilated(
        source[None],
        grad_out[None],
        (dilation, dilation),
        "VALID",
        rhs_dilation=(stride, stride),
        dimension_numbers=("CNHW", "IOHW", "NCHW"),
        preferred_element_type=jnp.float32,
    )
    return jnp.transpose(summed, (1, 0, 2, 3))


def flipped(kernel):
    return jnp.transpose(kernel, (1, 0, 2, 3))[:, :, ::-1, ::-1]


def spread_grad(grad_out, kernel):
    return lax.conv_general_dilated(
        grad_out[None],
        flipped(kernel),
        (1, 1),
        ((2, 2), (2, 2)),
        lhs_dilation=(2, 2),
        dimension_numbers=numbers,
        preferred_element_type=jnp.float32,
    )[0]


def silu_slope(pre_value):
    sigmoid_value = jax.nn.sigmoid(pre_value)
    return sigmoid_value * (1.0 + pre_value * (1.0 - sigmoid_value))


def normed_update(kernel, moment, gradient, mean_square):
    moment = momentum_rate * moment + gradient / jnp.sqrt(mean_square + mean_epsilon)
    return (kernel - learn_rate * moment, moment)


def body(image, perturb, target, kernel_one, kernel_two, moment_one, moment_two):
    target_wide = target.astype(jnp.float32)
    learned = [kernel_one, moment_one, kernel_two, moment_two]
    fast_one = kernel_one.astype(jnp.bfloat16)
    fast_two = kernel_two.astype(jnp.bfloat16)
    predict = jnp.zeros(target.shape, jnp.float32)
    for replay in range(REPLAYS):
        attacked = (image.astype(jnp.float32) + perturb).astype(jnp.bfloat16)
        beside_all = with_halo(attacked, (("rows", 1), ("cols", 2)), 2)
        hidden_pre = plain_conv(beside_all, fast_one, 1, 2)
        hidden = jax.nn.silu(hidden_pre).astype(jnp.bfloat16)
        left_col = shifted(hidden[:, :, -1:], "cols", 1)
        widened = jnp.concatenate([left_col, hidden], axis=2)
        top_row = shifted(widened[:, -1:, :], "rows", 1)
        extended = jnp.concatenate([top_row, widened], axis=1)
        predict = plain_conv(extended, fast_two, 2, 1)
        residual = (predict - target_wide).astype(jnp.bfloat16)
        grad_two = kernel_grad(extended, residual, 2, 1)
        grad_two = lax.psum(grad_two, ("rows", "cols"))
        spread = spread_grad(residual, fast_two)
        from_below = shifted(spread[:, :1, :].astype(jnp.bfloat16), "rows", -1).astype(jnp.float32)
        widened_grad = spread[:, 1:, :].at[:, -1:, :].add(from_below)
        from_right = shifted(widened_grad[:, :, :1], "cols", -1)
        hidden_grad = widened_grad[:, :, 1:].at[:, :, -1:].add(from_right)
        pre_grad = (hidden_grad * silu_slope(hidden_pre)).astype(jnp.bfloat16)
        grad_rimmed = with_halo(pre_grad, (("rows", 1), ("cols", 2)), 2)
        input_grad = plain_conv(grad_rimmed, flipped(fast_one), 1, 2)
        grad_one = kernel_grad(beside_all, pre_grad, 1, 2)
        perturb = jnp.clip(perturb + step_size * jnp.tanh(input_grad), -clip_bound, clip_bound)
        grad_one = lax.psum(grad_one, ("rows", "cols"))
        new_one, new_moment_one = normed_update(
            learned[0], learned[1], grad_one, jnp.mean(grad_one * grad_one)
        )
        new_two, new_moment_two = normed_update(
            learned[2], learned[3], grad_two, jnp.mean(grad_two * grad_two)
        )
        learned = [new_one, new_moment_one, new_two, new_moment_two]
        fast_one = new_one.astype(jnp.bfloat16)
        fast_two = new_two.astype(jnp.bfloat16)
    return (perturb, predict.astype(jnp.bfloat16), learned[0], learned[2], learned[1], learned[3])


def solution(mesh):
    in_specs = (
        P(None, "rows", "cols"),
        P(None, "rows", "cols"),
        P(None, "rows", "cols"),
        P(),
        P(),
        P(),
        P(),
    )
    out_specs = (P(None, "rows", "cols"), P(None, "rows", "cols"), P(), P(), P(), P())
    return jax.shard_map(body, mesh=mesh, in_specs=in_specs, out_specs=out_specs, check_vma=False)
```

profile of v0, /device:TPU:8, one launch (start us, length us, event | category | flops | bytes accessed | tf_op | source)
XLA Modules:
  0.0 782.5 jit_solution(5333286303783374361)
XLA Ops:
  19.6 3.4 collective-permute-start.2
  28.6 7.8 collective-permute-done.3
  80.5 5.1 scatter-add.20
  93.5 4.9 copy.320
  98.4 4.7 copy.329
  106.5 5.5 collective-permute-start.8
  113.3 5.5 fusion.109
  120.1 3.6 collective-permute-start.10
  123.7 3.5 collective-permute-start.11
  127.2 14.8 %fusion.22 = f32[48,48,3,3]{0,1,3,2:T(8,128)} fusion(bf16[1,48,20,260]{1,0,3,2:T(2,128)(2,1)} %copy.320, bf16[1,48,16,256]{1,2,3,0:T(8,128)(2,1)S(1)} %bitcast.267), kind=kOutput, calls=%fused_computation.48 | convolution fusion | flops 169869312 | bytes 975360 | tf_op jit(solution)/shard_map/transpose | solution.py:56
  158.1 113.7 %all-reduce.11.cloned.1.call-done = (f32[48,48,3,3]{0,1,3,2:T(8,128)}, f32[48,48,3,3]{0,1,3,2:T(8,128)}) async-done(((f32[48,48,3,3]{0,1,3,2:T(8,128)}, f32[48,48,3,3]{0,1,3,2:T(8,128)}), (f32[48,48,3,3]{0,1,3,2:T(8,128)}, f32[48,48,3,3]{0,1,3,2:T(8,128)})) %all-reduce.11.cloned.1.call-update) | async-done | bytes 165904 | tf_op jit(solution)/shard_map/psum | solution.py:114
  282.9 4.1 collective-permute-done.14
  310.3 3.5 reshape.229
  329.9 5.1 scatter-add.24
  337.6 4.9 copy.348
  342.5 4.7 copy.355
  350.6 6.2 collective-permute-start.20
  358.1 5.5 fusion.107
  364.9 3.6 collective-permute-start.22
  371.8 14.8 %fusion.20 = f32[48,48,3,3]{0,1,3,2:T(8,128)} fusion(bf16[1,48,20,260]{1,0,3,2:T(2,128)(2,1)} %copy.348, bf16[1,48,16,256]{1,2,3,0:T(8,128)(2,1)S(1)} %bitcast.268), kind=kOutput, calls=%fused_computation.46 | convolution fusion | flops 169869312 | bytes 975360 | tf_op jit(solution)/shard_map/transpose | solution.py:56
  403.4 112.0 %all-reduce.9.cloned.1.call-done = (f32[48,48,3,3]{0,1,3,2:T(8,128)}, f32[48,48,3,3]{0,1,3,2:T(8,128)}) async-done(((f32[48,48,3,3]{0,1,3,2:T(8,128)}, f32[48,48,3,3]{0,1,3,2:T(8,128)}), (f32[48,48,3,3]{0,1,3,2:T(8,128)}, f32[48,48,3,3]{0,1,3,2:T(8,128)})) %all-reduce.9.cloned.1.call-update) | async-done | bytes 165904 | tf_op jit(solution)/shard_map/psum | solution.py:114
  527.4 4.2 collective-permute-done.26
  540.3 3.9 convolution_select_fusion.3
  574.5 4.9 copy.368
  579.4 3.5 slice.414
  582.9 4.7 copy.370
  589.0 5.1 scatter-add.26
  596.7 7.1 fusion.105
  605.0 4.8 collective-permute-start.32
  615.3 3.9 collective-permute-start.34
  622.2 14.8 %fusion.18 = f32[48,48,3,3]{0,1,3,2:T(8,128)} fusion(bf16[1,48,20,260]{1,0,3,2:T(2,128)(2,1)} %copy.368, bf16[1,48,16,256]{1,2,3,0:T(8,128)(2,1)S(1)} %bitcast.269), kind=kOutput, calls=%fused_computation.44 | convolution fusion | flops 169869312 | bytes 975360 | tf_op jit(solution)/shard_map/transpose | solution.py:56
  650.2 117.2 %all-reduce.7.cloned.1.call-done = (f32[48,48,3,3]{0,1,3,2:T(8,128)}, f32[48,48,3,3]{0,1,3,2:T(8,128)}) async-done(((f32[48,48,3,3]{0,1,3,2:T(8,128)}, f32[48,48,3,3]{0,1,3,2:T(8,128)}), (f32[48,48,3,3]{0,1,3,2:T(8,128)}, f32[48,48,3,3]{0,1,3,2:T(8,128)})) %all-reduce.7.cloned.1.call-update) | async-done | bytes 165904 | tf_op jit(solution)/shard_map/psum | solution.py:114
  (388 shorter events, 251.1 us)
Async XLA Ops:
  7.2 264.7 %all-reduce.11.cloned.1.call-start = ((), (), s32[]{:S(2)}) async-start(), calls=%async_computation.2 | async-start | bytes 884736 | tf_op jit(solution)/shard_map/psum | solution.py:114
  19.6 9.0 %collective-permute-start.2 = (bf16[48,20,2]{2,0,1:T(8,128)(2,1)S(1)}, bf16[48,20,2]{2,0,1:T(8,128)(2,1)S(1)}, u32[]{:S(2)}, u32[]{:S(2)}) collective-permute-start(bf16[48,20,2]{2,0,1:T(8,128)(2,1)S(1)} %get-tuple-element.162), channel_id=1, source_target_pairs={{0,1},{1,2},{2,3},{3,4},{4,5},{5,6},{6,7},{8,9},{9,10},{10,11},{11... | collective-permute-start | bytes 11528 | tf_op jit(solution)/shard_map/ppermute | solution.py:20
  23.0 13.4 %collective-permute-start.3 = (bf16[48,20,2]{2,0,1:T(8,128)(2,1)S(1)}, bf16[48,20,2]{2,0,1:T(8,128)(2,1)S(1)}, u32[]{:S(2)}, u32[]{:S(2)}) collective-permute-start(bf16[48,20,2]{2,0,1:T(8,128)(2,1)S(1)} %get-tuple-element.163), channel_id=1, source_target_pairs={{1,0},{2,1},{3,2},{4,3},{5,4},{6,5},{7,6},{9,8},{10,9},{11,10},{12... | collective-permute-start | bytes 11528 | tf_op jit(solution)/shard_map/ppermute | solution.py:23
  46.2 6.4 collective-permute-start.4
  53.4 5.7 collective-permute-start.5
  86.3 18.5 %collective-permute-start.7 = (f32[48,16,1]{0,1,2:T(8,128)S(1)}, f32[48,16,1]{0,1,2:T(8,128)S(1)}, u32[]{:S(2)}, u32[]{:S(2)}) collective-permute-start(f32[48,16,1]{0,1,2:T(8,128)S(1)} %slice.369), channel_id=1, source_target_pairs={{1,0},{2,1},{3,2},{4,3},{5,4},{6,5},{7,6},{9,8},{10,9},{11,10},{12... | collective-permute-start | bytes 9224 | tf_op jit(solution)/shard_map/ppermute | solution.py:31
  106.5 13.2 %collective-permute-start.8 = (bf16[48,2,256]{0,1,2:T(2,128)(2,1)S(1)}, bf16[48,2,256]{0,1,2:T(2,128)(2,1)S(1)}, u32[]{:S(2)}, u32[]{:S(2)}) collective-permute-start(bf16[48,2,256]{0,1,2:T(2,128)(2,1)S(1)} %get-tuple-element.130), channel_id=1, source_target_pairs={{0,8},{8,16},{16,24},{1,9},{9,17},{17,25},{2,10},{10,18},{18,26},{... | collective-permute-start | bytes 147464 | tf_op jit(solution)/shard_map/ppermute | solution.py:20
  112.0 7.8 collective-permute-start.9
  120.1 22.2 %collective-permute-start.10 = (bf16[48,20,2]{2,0,1:T(8,128)(2,1)S(1)}, bf16[48,20,2]{2,0,1:T(8,128)(2,1)S(1)}, u32[]{:S(2)}, u32[]{:S(2)}) collective-permute-start(bf16[48,20,2]{2,0,1:T(8,128)(2,1)S(1)} %get-tuple-element.160), channel_id=1, source_target_pairs={{0,1},{1,2},{2,3},{3,4},{4,5},{5,6},{6,7},{8,9},{9,10},{10,11},{11... | collective-permute-start | bytes 11528 | tf_op jit(solution)/shard_map/ppermute | solution.py:20
  123.7 18.5 %collective-permute-start.11 = (bf16[48,20,2]{2,0,1:T(8,128)(2,1)S(1)}, bf16[48,20,2]{2,0,1:T(8,128)(2,1)S(1)}, u32[]{:S(2)}, u32[]{:S(2)}) collective-permute-start(bf16[48,20,2]{2,0,1:T(8,128)(2,1)S(1)} %get-tuple-element.161), channel_id=1, source_target_pairs={{1,0},{2,1},{3,2},{4,3},{5,4},{6,5},{7,6},{9,8},{10,9},{11,10},{12... | collective-permute-start | bytes 11528 | tf_op jit(solution)/shard_map/ppermute | solution.py:23
  142.0 373.5 %all-reduce.9.cloned.1.call-start = ((), (), s32[]{:S(2)}) async-start(), calls=%async_computation.1 | async-start | bytes 884736 | tf_op jit(solution)/shard_map/psum | solution.py:114
  154.3 120.0 %collective-permute-start.12 = (bf16[48,2,256]{0,1,2:T(2,128)(2,1)S(1)}, bf16[48,2,256]{0,1,2:T(2,128)(2,1)S(1)}, u32[]{:S(2)}, u32[]{:S(2)}) collective-permute-start(bf16[48,2,256]{0,1,2:T(2,128)(2,1)S(1)} %get-tuple-element.128), channel_id=1, source_target_pairs={{0,8},{8,16},{16,24},{1,9},{9,17},{17,25},{2,10},{10,18},{18,26},{... | collective-permute-start | bytes 147464 | tf_op jit(solution)/shard_map/ppermute | solution.py:20
  156.8 117.6 %collective-permute-start.13 = (bf16[48,2,256]{0,1,2:T(2,128)(2,1)S(1)}, bf16[48,2,256]{0,1,2:T(2,128)(2,1)S(1)}, u32[]{:S(2)}, u32[]{:S(2)}) collective-permute-start(bf16[48,2,256]{0,1,2:T(2,128)(2,1)S(1)} %get-tuple-element.129), channel_id=1, source_target_pairs={{8,0},{16,8},{24,16},{9,1},{17,9},{25,17},{10,2},{18,10},{26,18},{... | collective-permute-start | bytes 147464 | tf_op jit(solution)/shard_map/ppermute | solution.py:23
  274.7 12.3 %collective-permute-start.14 = (bf16[48,20,2]{2,0,1:T(8,128)(2,1)S(1)}, bf16[48,20,2]{2,0,1:T(8,128)(2,1)S(1)}, u32[]{:S(2)}, u32[]{:S(2)}) collective-permute-start(bf16[48,20,2]{2,0,1:T(8,128)(2,1)S(1)} %get-tuple-element.158), channel_id=1, source_target_pairs={{0,1},{1,2},{2,3},{3,4},{4,5},{5,6},{6,7},{8,9},{9,10},{10,11},{11... | collective-permute-start | bytes 11528 | tf_op jit(solution)/shard_map/ppermute | solution.py:20
  278.1 10.6 %collective-permute-start.15 = (bf16[48,20,2]{2,0,1:T(8,128)(2,1)S(1)}, bf16[48,20,2]{2,0,1:T(8,128)(2,1)S(1)}, u32[]{:S(2)}, u32[]{:S(2)}) collective-permute-start(bf16[48,20,2]{2,0,1:T(8,128)(2,1)S(1)} %get-tuple-element.159), channel_id=1, source_target_pairs={{1,0},{2,1},{3,2},{4,3},{5,4},{6,5},{7,6},{9,8},{10,9},{11,10},{12... | collective-permute-start | bytes 11528 | tf_op jit(solution)/shard_map/ppermute | solution.py:23
  298.4 6.4 collective-permute-start.16
  335.6 13.3 %collective-permute-start.19 = (f32[48,16,1]{0,1,2:T(8,128)S(1)}, f32[48,16,1]{0,1,2:T(8,128)S(1)}, u32[]{:S(2)}, u32[]{:S(2)}) collective-permute-start(f32[48,16,1]{0,1,2:T(8,128)S(1)} %slice.394), channel_id=1, source_target_pairs={{1,0},{2,1},{3,2},{4,3},{5,4},{6,5},{7,6},{9,8},{10,9},{11,10},{12... | collective-permute-start | bytes 9224 | tf_op jit(solution)/shard_map/ppermute | solution.py:31
  350.6 13.9 %collective-permute-start.20 = (bf16[48,2,256]{0,1,2:T(2,128)(2,1)S(1)}, bf16[48,2,256]{0,1,2:T(2,128)(2,1)S(1)}, u32[]{:S(2)}, u32[]{:S(2)}) collective-permute-start(bf16[48,2,256]{0,1,2:T(2,128)(2,1)S(1)} %get-tuple-element.126), channel_id=1, source_target_pairs={{0,8},{8,16},{16,24},{1,9},{9,17},{17,25},{2,10},{10,18},{18,26},{... | collective-permute-start | bytes 147464 | tf_op jit(solution)/shard_map/ppermute | solution.py:20
  356.8 7.8 collective-permute-start.21
  364.9 22.2 %collective-permute-start.22 = (bf16[48,20,2]{2,0,1:T(8,128)(2,1)S(1)}, bf16[48,20,2]{2,0,1:T(8,128)(2,1)S(1)}, u32[]{:S(2)}, u32[]{:S(2)}) collective-permute-start(bf16[48,20,2]{2,0,1:T(8,128)(2,1)S(1)} %get-tuple-element.156), channel_id=1, source_target_pairs={{0,1},{1,2},{2,3},{3,4},{4,5},{5,6},{6,7},{8,9},{9,10},{10,11},{11... | collective-permute-start | bytes 11528 | tf_op jit(solution)/shard_map/ppermute | solution.py:20
  368.5 18.5 %collective-permute-start.23 = (bf16[48,20,2]{2,0,1:T(8,128)(2,1)S(1)}, bf16[48,20,2]{2,0,1:T(8,128)(2,1)S(1)}, u32[]{:S(2)}, u32[]{:S(2)}) collective-permute-start(bf16[48,20,2]{2,0,1:T(8,128)(2,1)S(1)} %get-tuple-element.157), channel_id=1, source_target_pairs={{1,0},{2,1},{3,2},{4,3},{5,4},{6,5},{7,6},{9,8},{10,9},{11,10},{12... | collective-permute-start | bytes 11528 | tf_op jit(solution)/shard_map/ppermute | solution.py:23
  386.6 380.8 %all-reduce.7.cloned.1.call-start = ((), (), s32[]{:S(2)}) async-start(), calls=%async_computation | async-start | bytes 884736 | tf_op jit(solution)/shard_map/psum | solution.py:114
  399.6 119.2 %collective-permute-start.24 = (bf16[48,2,256]{0,1,2:T(2,128)(2,1)S(1)}, bf16[48,2,256]{0,1,2:T(2,128)(2,1)S(1)}, u32[]{:S(2)}, u32[]{:S(2)}) collective-permute-start(bf16[48,2,256]{0,1,2:T(2,128)(2,1)S(1)} %get-tuple-element.124), channel_id=1, source_target_pairs={{0,8},{8,16},{16,24},{1,9},{9,17},{17,25},{2,10},{10,18},{18,26},{... | collective-permute-start | bytes 147464 | tf_op jit(solution)/shard_map/ppermute | solution.py:20
  402.1 116.8 %collective-permute-start.25 = (bf16[48,2,256]{0,1,2:T(2,128)(2,1)S(1)}, bf16[48,2,256]{0,1,2:T(2,128)(2,1)S(1)}, u32[]{:S(2)}, u32[]{:S(2)}) collective-permute-start(bf16[48,2,256]{0,1,2:T(2,128)(2,1)S(1)} %get-tuple-element.125), channel_id=1, source_target_pairs={{8,0},{16,8},{24,16},{9,1},{17,9},{25,17},{10,2},{18,10},{26,18},{... | collective-permute-start | bytes 147464 | tf_op jit(solution)/shard_map/ppermute | solution.py:23
  519.3 12.3 %collective-permute-start.26 = (bf16[48,20,2]{2,0,1:T(8,128)(2,1)S(1)}, bf16[48,20,2]{2,0,1:T(8,128)(2,1)S(1)}, u32[]{:S(2)}, u32[]{:S(2)}) collective-permute-start(bf16[48,20,2]{2,0,1:T(8,128)(2,1)S(1)} %get-tuple-element.154), channel_id=1, source_target_pairs={{0,1},{1,2},{2,3},{3,4},{4,5},{5,6},{6,7},{8,9},{9,10},{10,11},{11... | collective-permute-start | bytes 11528 | tf_op jit(solution)/shard_map/ppermute | solution.py:20
  522.6 10.6 %collective-permute-start.27 = (bf16[48,20,2]{2,0,1:T(8,128)(2,1)S(1)}, bf16[48,20,2]{2,0,1:T(8,128)(2,1)S(1)}, u32[]{:S(2)}, u32[]{:S(2)}) collective-permute-start(bf16[48,20,2]{2,0,1:T(8,128)(2,1)S(1)} %get-tuple-element.155), channel_id=1, source_target_pairs={{1,0},{2,1},{3,2},{4,3},{5,4},{6,5},{7,6},{9,8},{10,9},{11,10},{12... | collective-permute-start | bytes 11528 | tf_op jit(solution)/shard_map/ppermute | solution.py:23
  545.2 6.4 collective-permute-start.28
  573.2 14.4 %collective-permute-start.30 = (bf16[48,1,257]{0,1,2:T(2,128)(2,1)}, bf16[48,1,257]{0,1,2:T(2,128)(2,1)}, u32[]{:S(2)}, u32[]{:S(2)}) collective-permute-start(bf16[48,1,257]{0,1,2:T(2,128)(2,1)} %slice.527), channel_id=1, source_target_pairs={{8,0},{16,8},{24,16},{9,1},{17,9},{25,17},{10,2},{18,10},{26,18},{... | collective-permute-start | bytes 74024 | tf_op jit(solution)/shard_map/ppermute | solution.py:31
  594.8 9.2 %collective-permute-start.31 = (f32[48,16,1]{0,1,2:T(8,128)S(1)}, f32[48,16,1]{0,1,2:T(8,128)S(1)}, u32[]{:S(2)}, u32[]{:S(2)}) collective-permute-start(f32[48,16,1]{0,1,2:T(8,128)S(1)} %slice.419), channel_id=1, source_target_pairs={{1,0},{2,1},{3,2},{4,3},{5,4},{6,5},{7,6},{9,8},{10,9},{11,10},{12... | collective-permute-start | bytes 9224 | tf_op jit(solution)/shard_map/ppermute | solution.py:31
  605.0 8.9 %collective-permute-start.32 = (bf16[48,2,256]{0,1,2:T(2,128)(2,1)S(1)}, bf16[48,2,256]{0,1,2:T(2,128)(2,1)S(1)}, u32[]{:S(2)}, u32[]{:S(2)}) collective-permute-start(bf16[48,2,256]{0,1,2:T(2,128)(2,1)S(1)} %get-tuple-element.122), channel_id=1, source_target_pairs={{0,8},{8,16},{16,24},{1,9},{9,17},{17,25},{2,10},{10,18},{18,26},{... | collective-permute-start | bytes 147464 | tf_op jit(solution)/shard_map/ppermute | solution.py:20
  615.3 21.8 %collective-permute-start.34 = (bf16[48,20,2]{2,0,1:T(8,128)(2,1)S(1)}, bf16[48,20,2]{2,0,1:T(8,128)(2,1)S(1)}, u32[]{:S(2)}, u32[]{:S(2)}) collective-permute-start(bf16[48,20,2]{2,0,1:T(8,128)(2,1)S(1)} %get-tuple-element.152), channel_id=1, source_target_pairs={{0,1},{1,2},{2,3},{3,4},{4,5},{5,6},{6,7},{8,9},{9,10},{10,11},{11... | collective-permute-start | bytes 11528 | tf_op jit(solution)/shard_map/ppermute | solution.py:20
  619.2 17.8 %collective-permute-start.35 = (bf16[48,20,2]{2,0,1:T(8,128)(2,1)S(1)}, bf16[48,20,2]{2,0,1:T(8,128)(2,1)S(1)}, u32[]{:S(2)}, u32[]{:S(2)}) collective-permute-start(bf16[48,20,2]{2,0,1:T(8,128)(2,1)S(1)} %get-tuple-element.153), channel_id=1, source_target_pairs={{1,0},{2,1},{3,2},{4,3},{5,4},{6,5},{7,6},{9,8},{10,9},{11,10},{12... | collective-permute-start | bytes 11528 | tf_op jit(solution)/shard_map/ppermute | solution.py:23
  (75 other events, 1475.2 us)
Sparse Core Ops, SparseCore 0:
  142.1 129.6 all-reduce.10
  386.7 128.7 all-reduce.8
  637.1 130.2 all-reduce.6
where the time goes:
time: 792 us; the launch traced here: 782 us
  waiting for transfers between devices  378 us (48%)
  local copies, waits for them, and re-layouts  163 us (21%)
  starting transfers between devices  95.5 us (12%)
  matrix products  89.8 us (11%)
  other arithmetic  35.4 us (4%)
  between operations  20.5 us (3%)
    psum x3, waiting for transfers between devices, body(): grad_one = lax.psum(grad_one, ('rows', 'cols'))  343 us
    transpose x6, matrix products, kernel_grad(): return jnp.transpose(summed, (1, 0, 2, 3))  62.4 us
    conv_general_dilated x33, local copies, waits for them, and re-layouts, plain_conv(): lax.conv_general_dilated(source[None], kernel, (stride, stride), 'VALID',...  54.5 us
    ppermute x12, starting transfers between devices, with_halo(): lax.ppermute(lax.slice_in_dim(block, block.shape[dim] - width, None, axis...  44.4 us
    broadcast_in_dim x15, local copies, waits for them, and re-layouts, plain_conv(): source[None]  32 us
    ppermute x12, starting transfers between devices, with_halo(): lax.ppermute(lax.slice_in_dim(block, 0, width, axis=dim), axis, backward)  27.7 us
    unnamed x149, local copies, waits for them, and re-layouts  26.4 us
    conv_general_dilated x9, matrix products, plain_conv(): lax.conv_general_dilated(source[None], kernel, (stride, stride), 'VALID',...  23.4 us
  transfers between devices with their start and end apart: 39, of which 16 were waited for; matrix products, arithmetic and copies ran while one was open for 20% of the time, Pallas kernels for 0%

commit v1 on v0

--- a/solution.py
+++ b/solution.py
@@ -111,7 +111,7 @@
         input_grad = plain_conv(grad_rimmed, flipped(fast_one), 1, 2)
         grad_one = kernel_grad(beside_all, pre_grad, 1, 2)
         perturb = jnp.clip(perturb + step_size * jnp.tanh(input_grad), -clip_bound, clip_bound)
-        grad_one = lax.psum(grad_one, ("rows", "cols"))
+        grad_one = jnp.sum(lax.all_gather(grad_one, ("rows", "cols")), axis=0)
         new_one, new_moment_one = normed_update(
             learned[0], learned[1], grad_one, jnp.mean(grad_one * grad_one)
         )

time: 792 us -> 921 us (1.16)
  waiting for transfers between devices: 378 us -> 483 us
  other arithmetic: 35.4 us -> 54.6 us
  local copies, waits for them, and re-layouts: 163 us -> 175 us
    all_gather x0 -> x3, waiting for transfers between devices: none -> 204 us  [body(): grad_one = jnp.sum(lax.all_gather(grad_one, ('rows', 'cols')), axis=0)]
    psum x3, waiting for transfers between devices: 343 us -> 226 us  [body(): grad_two = lax.psum(grad_two, ('rows', 'cols'))]
    ppermute x12, waiting for transfers between devices: 13.2 us -> 32.4 us  [with_halo(): lax.ppermute(lax.slice_in_dim(block, 0, width, axis=dim), axis, backward)]
    reduce_sum x0 -> x3, other arithmetic: none -> 17.7 us  [body(): grad_one = jnp.sum(lax.all_gather(grad_one, ('rows', 'cols')), axis=0)]
    unnamed x149 -> x155, local copies, waits for them, and re-layouts: 26.4 us -> 29.1 us
  transfers between devices with their start and end apart: 39 -> 42, of which waited for: 16 -> 21; matrix products, arithmetic and copies ran while one was open for 20% -> 20% of each run, Pallas kernels for 0% -> 0%
where the time goes in v1:
time: 921 us; the launch traced here: 910 us
  waiting for transfers between devices  483 us (52%)
  local copies, waits for them, and re-layouts  175 us (19%)
  starting transfers between devices  92.8 us (10%)
  matrix products  83.8 us (9%)
  other arithmetic  54.6 us (6%)
  between operations  20.8 us (2%)
    psum x3, waiting for transfers between devices, body(): grad_two = lax.psum(grad_two, ('rows', 'cols'))  226 us
    all_gather x3, waiting for transfers between devices, body(): grad_one = jnp.sum(lax.all_gather(grad_one, ('rows', 'cols')), axis=0)  204 us
    transpose x6, matrix products, kernel_grad(): return jnp.transpose(summed, (1, 0, 2, 3))  57.8 us
    conv_general_dilated x33, local copies, waits for them, and re-layouts, plain_conv(): lax.conv_general_dilated(source[None], kernel, (stride, stride), 'VALID',...  54.3 us
    ppermute x12, starting transfers between devices, with_halo(): lax.ppermute(lax.slice_in_dim(block, block.shape[dim] - width, None, axis...  38.2 us
    ppermute x12, waiting for transfers between devices, with_halo(): lax.ppermute(lax.slice_in_dim(block, 0, width, axis=dim), axis, backward)  32.4 us
    broadcast_in_dim x15, local copies, waits for them, and re-layouts, plain_conv(): source[None]  32.1 us
    unnamed x155, local copies, waits for them, and re-layouts  29.1 us
  transfers between devices with their start and end apart: 42, of which 21 were waited for; matrix products, arithmetic and copies ran while one was open for 20% of the time, Pallas kernels for 0%

profile of v1, /device:TPU:8, one launch (start us, length us, event | category | flops | bytes accessed | tf_op | source)
XLA Modules:
  0.0 910.0 jit_solution(5821307801060761890)
XLA Ops:
  28.6 7.8 collective-permute-done.3
  79.6 5.0 copy.412
  88.0 4.7 copy.423
  94.1 5.1 scatter-add.20
  101.9 6.9 fusion.109
  113.5 12.3 %fusion.22 = f32[48,48,3,3]{0,1,3,2:T(8,128)S(1)} fusion(bf16[1,48,20,260]{1,0,3,2:T(2,128)(2,1)S(1)} %copy-done.24, bf16[1,48,16,256]{1,2,3,0:T(8,128)(2,1)S(1)} %bitcast.273), kind=kOutput, calls=%fused_computation.48 | convolution fusion | flops 169869312 | bytes 975360 | tf_op jit(solution)/shard_map/transpose | solution.py:56
  144.2 8.3 collective-permute-done.11
  172.6 4.0 collective-permute-start.15
  176.6 62.5 %all-reduce.4.cloned.1.call-done = f32[48,48,3,3]{0,1,3,2:T(8,128)} async-done(((f32[48,48,3,3]{0,1,3,2:T(8,128)}), f32[48,48,3,3]{0,1,3,2:T(8,128)}) %all-reduce.4.cloned.1.call-update) | async-done | bytes 82960 | tf_op jit(solution)/shard_map/psum | solution.py:103
  248.6 74.6 %all-gather.7.cloned.1.call-done = f32[1536,48,3,3]{1,3,2,0:T(4,128)} async-done(((f32[48,48,3,3]{1,3,2,0:T(4,128)}), f32[1536,48,3,3]{1,3,2,0:T(4,128)}) %all-gather.7.cloned.1.call-update) | async-done | bytes 2654224 | tf_op jit(solution)/shard_map/all_gather | solution.py:114
  323.1 5.9 reduce_sum.81
  364.5 5.0 copy.442
  372.9 4.7 copy.451
  379.0 5.1 scatter-add.24
  387.3 6.9 fusion.107
  398.7 12.3 %fusion.20 = f32[48,48,3,3]{0,1,3,2:T(8,128)S(1)} fusion(bf16[1,48,20,260]{1,0,3,2:T(2,128)(2,1)S(1)} %copy-done.25, bf16[1,48,16,256]{1,2,3,0:T(8,128)(2,1)S(1)} %bitcast.274), kind=kOutput, calls=%fused_computation.46 | convolution fusion | flops 169869312 | bytes 975360 | tf_op jit(solution)/shard_map/transpose | solution.py:56
  412.1 4.1 collective-permute-start.20
  430.4 8.0 collective-permute-done.23
  459.0 4.3 collective-permute-start.27
  463.3 61.2 %all-reduce.6.cloned.1.call-done = f32[48,48,3,3]{0,1,3,2:T(8,128)} async-done(((f32[48,48,3,3]{0,1,3,2:T(8,128)}), f32[48,48,3,3]{0,1,3,2:T(8,128)}) %all-reduce.6.cloned.1.call-update) | async-done | bytes 82960 | tf_op jit(solution)/shard_map/psum | solution.py:103
  533.0 75.4 %all-gather.9.cloned.1.call-done = f32[1536,48,3,3]{1,3,2,0:T(4,128)} async-done(((f32[48,48,3,3]{1,3,2,0:T(4,128)}), f32[1536,48,3,3]{1,3,2,0:T(4,128)}) %all-gather.9.cloned.1.call-update) | async-done | bytes 2654224 | tf_op jit(solution)/shard_map/all_gather | solution.py:114
  608.4 5.9 reduce_sum.84
  649.7 4.9 copy.464
  658.1 4.7 copy.468
  664.2 5.1 scatter-add.26
  672.4 6.9 fusion.105
  683.9 12.3 %fusion.18 = f32[48,48,3,3]{0,1,3,2:T(8,128)S(1)} fusion(bf16[1,48,20,260]{1,0,3,2:T(2,128)(2,1)S(1)} %copy-done.23, bf16[1,48,16,256]{1,2,3,0:T(8,128)(2,1)S(1)} %bitcast.275), kind=kOutput, calls=%fused_computation.44 | convolution fusion | flops 169869312 | bytes 975360 | tf_op jit(solution)/shard_map/transpose | solution.py:56
  700.3 4.1 collective-permute-start.32
  705.7 102.3 %all-reduce.8.cloned.1.call-done = f32[48,48,3,3]{0,1,3,2:T(8,128)} async-done(((f32[48,48,3,3]{0,1,3,2:T(8,128)}), f32[48,48,3,3]{0,1,3,2:T(8,128)}) %all-reduce.8.cloned.1.call-update) | async-done | bytes 82960 | tf_op jit(solution)/shard_map/psum | solution.py:103
  819.3 5.9 collective-permute-done.34
  839.5 53.9 %all-gather.11.cloned.1.call-done = f32[1536,48,3,3]{1,3,2,0:T(4,128)} async-done(((f32[48,48,3,3]{1,3,2,0:T(4,128)}), f32[1536,48,3,3]{1,3,2,0:T(4,128)}) %all-gather.11.cloned.1.call-update) | async-done | bytes 2654224 | tf_op jit(solution)/shard_map/all_gather | solution.py:114
  893.5 5.9 reduce_sum.87
  (413 shorter events, 293.0 us)
Async XLA Ops:
  7.2 231.9 %all-reduce.4.cloned.1.call-start = ((), (), s32[]{:S(2)}) async-start(), calls=%async_computation | async-start | bytes 442368 | tf_op jit(solution)/shard_map/psum | solution.py:103
  19.6 9.0 collective-permute-start.2
  23.0 13.4 %collective-permute-start.3 = (bf16[48,20,2]{2,0,1:T(8,128)(2,1)S(1)}, bf16[48,20,2]{2,0,1:T(8,128)(2,1)S(1)}, u32[]{:S(2)}, u32[]{:S(2)}) collective-permute-start(bf16[48,20,2]{2,0,1:T(8,128)(2,1)S(1)} %get-tuple-element.163), channel_id=1, source_target_pairs={{1,0},{2,1},{3,2},{4,3},{5,4},{6,5},{7,6},{9,8},{10,9},{11,10},{12... | collective-permute-start | bytes 11528 | tf_op jit(solution)/shard_map/ppermute | solution.py:23
  46.1 6.4 collective-permute-start.4
  53.3 5.7 collective-permute-start.5
  78.3 14.4 %collective-permute-start.6 = (bf16[48,1,257]{0,1,2:T(2,128)(2,1)S(1)}, bf16[48,1,257]{0,1,2:T(2,128)(2,1)S(1)}, u32[]{:S(2)}, u32[]{:S(2)}) collective-permute-start(bf16[48,1,257]{0,1,2:T(2,128)(2,1)S(1)} %slice.529), channel_id=1, source_target_pairs={{8,0},{16,8},{24,16},{9,1},{17,9},{25,17},{10,2},{18,10},{26,18},{... | collective-permute-start | bytes 74024 | tf_op jit(solution)/shard_map/ppermute | solution.py:31
  99.9 11.1 %collective-permute-start.7 = (f32[48,16,1]{0,1,2:T(8,128)S(1)}, f32[48,16,1]{0,1,2:T(8,128)S(1)}, u32[]{:S(2)}, u32[]{:S(2)}) collective-permute-start(f32[48,16,1]{0,1,2:T(8,128)S(1)} %slice.369), channel_id=1, source_target_pairs={{1,0},{2,1},{3,2},{4,3},{5,4},{6,5},{7,6},{9,8},{10,9},{11,10},{12... | collective-permute-start | bytes 9224 | tf_op jit(solution)/shard_map/ppermute | solution.py:31
  108.9 214.2 %all-gather.7.cloned.1.call-start = ((), (), s32[]{:S(2)}) async-start(), calls=%async_computation.3 | async-start | bytes 9732096 | tf_op jit(solution)/shard_map/all_gather | solution.py:114
  126.7 397.8 %all-reduce.6.cloned.1.call-start = ((), (), s32[]{:S(2)}) async-start(), calls=%async_computation.1 | async-start | bytes 442368 | tf_op jit(solution)/shard_map/psum | solution.py:103
  127.0 5.7 collective-permute-start.8
  135.2 9.0 collective-permute-start.10
  139.1 13.3 %collective-permute-start.11 = (bf16[48,20,2]{2,0,1:T(8,128)(2,1)S(1)}, bf16[48,20,2]{2,0,1:T(8,128)(2,1)S(1)}, u32[]{:S(2)}, u32[]{:S(2)}) collective-permute-start(bf16[48,20,2]{2,0,1:T(8,128)(2,1)S(1)} %get-tuple-element.161), channel_id=1, source_target_pairs={{1,0},{2,1},{3,2},{4,3},{5,4},{6,5},{7,6},{9,8},{10,9},{11,10},{12... | collective-permute-start | bytes 11528 | tf_op jit(solution)/shard_map/ppermute | solution.py:23
  169.7 71.7 %collective-permute-start.14 = (bf16[48,20,2]{2,0,1:T(8,128)(2,1)S(1)}, bf16[48,20,2]{2,0,1:T(8,128)(2,1)S(1)}, u32[]{:S(2)}, u32[]{:S(2)}) collective-permute-start(bf16[48,20,2]{2,0,1:T(8,128)(2,1)S(1)} %get-tuple-element.158), channel_id=1, source_target_pairs={{0,1},{1,2},{2,3},{3,4},{4,5},{5,6},{6,7},{8,9},{9,10},{10,11},{11... | collective-permute-start | bytes 11528 | tf_op jit(solution)/shard_map/ppermute | solution.py:20
  172.6 68.8 %collective-permute-start.15 = (bf16[48,20,2]{2,0,1:T(8,128)(2,1)S(1)}, bf16[48,20,2]{2,0,1:T(8,128)(2,1)S(1)}, u32[]{:S(2)}, u32[]{:S(2)}) collective-permute-start(bf16[48,20,2]{2,0,1:T(8,128)(2,1)S(1)} %get-tuple-element.159), channel_id=1, source_target_pairs={{1,0},{2,1},{3,2},{4,3},{5,4},{6,5},{7,6},{9,8},{10,9},{11,10},{12... | collective-permute-start | bytes 11528 | tf_op jit(solution)/shard_map/ppermute | solution.py:23
  335.0 6.4 collective-permute-start.16
  363.2 14.4 %collective-permute-start.18 = (bf16[48,1,257]{0,1,2:T(2,128)(2,1)}, bf16[48,1,257]{0,1,2:T(2,128)(2,1)}, u32[]{:S(2)}, u32[]{:S(2)}) collective-permute-start(bf16[48,1,257]{0,1,2:T(2,128)(2,1)} %slice.528), channel_id=1, source_target_pairs={{8,0},{16,8},{24,16},{9,1},{17,9},{25,17},{10,2},{18,10},{26,18},{... | collective-permute-start | bytes 74024 | tf_op jit(solution)/shard_map/ppermute | solution.py:31
  384.8 11.4 %collective-permute-start.19 = (f32[48,16,1]{0,1,2:T(8,128)S(1)}, f32[48,16,1]{0,1,2:T(8,128)S(1)}, u32[]{:S(2)}, u32[]{:S(2)}) collective-permute-start(f32[48,16,1]{0,1,2:T(8,128)S(1)} %slice.394), channel_id=1, source_target_pairs={{1,0},{2,1},{3,2},{4,3},{5,4},{6,5},{7,6},{9,8},{10,9},{11,10},{12... | collective-permute-start | bytes 9224 | tf_op jit(solution)/shard_map/ppermute | solution.py:31
  394.2 214.2 %all-gather.9.cloned.1.call-start = ((), (), s32[]{:S(2)}) async-start(), calls=%async_computation.4 | async-start | bytes 9732096 | tf_op jit(solution)/shard_map/all_gather | solution.py:114
  411.8 396.2 %all-reduce.8.cloned.1.call-start = ((), (), s32[]{:S(2)}) async-start(), calls=%async_computation.2 | async-start | bytes 442368 | tf_op jit(solution)/shard_map/psum | solution.py:103
  412.1 6.5 collective-permute-start.20
  421.5 9.0 collective-permute-start.22
  425.4 13.1 %collective-permute-start.23 = (bf16[48,20,2]{2,0,1:T(8,128)(2,1)S(1)}, bf16[48,20,2]{2,0,1:T(8,128)(2,1)S(1)}, u32[]{:S(2)}, u32[]{:S(2)}) collective-permute-start(bf16[48,20,2]{2,0,1:T(8,128)(2,1)S(1)} %get-tuple-element.157), channel_id=1, source_target_pairs={{1,0},{2,1},{3,2},{4,3},{5,4},{6,5},{7,6},{9,8},{10,9},{11,10},{12... | collective-permute-start | bytes 11528 | tf_op jit(solution)/shard_map/ppermute | solution.py:23
  456.2 70.7 %collective-permute-start.26 = (bf16[48,20,2]{2,0,1:T(8,128)(2,1)S(1)}, bf16[48,20,2]{2,0,1:T(8,128)(2,1)S(1)}, u32[]{:S(2)}, u32[]{:S(2)}) collective-permute-start(bf16[48,20,2]{2,0,1:T(8,128)(2,1)S(1)} %get-tuple-element.154), channel_id=1, source_target_pairs={{0,1},{1,2},{2,3},{3,4},{4,5},{5,6},{6,7},{8,9},{9,10},{10,11},{11... | collective-permute-start | bytes 11528 | tf_op jit(solution)/shard_map/ppermute | solution.py:20
  459.0 67.9 %collective-permute-start.27 = (bf16[48,20,2]{2,0,1:T(8,128)(2,1)S(1)}, bf16[48,20,2]{2,0,1:T(8,128)(2,1)S(1)}, u32[]{:S(2)}, u32[]{:S(2)}) collective-permute-start(bf16[48,20,2]{2,0,1:T(8,128)(2,1)S(1)} %get-tuple-element.155), channel_id=1, source_target_pairs={{1,0},{2,1},{3,2},{4,3},{5,4},{6,5},{7,6},{9,8},{10,9},{11,10},{12... | collective-permute-start | bytes 11528 | tf_op jit(solution)/shard_map/ppermute | solution.py:23
  620.3 6.4 collective-permute-start.28
  648.4 14.4 %collective-permute-start.30 = (bf16[48,1,257]{0,1,2:T(2,128)(2,1)}, bf16[48,1,257]{0,1,2:T(2,128)(2,1)}, u32[]{:S(2)}, u32[]{:S(2)}) collective-permute-start(bf16[48,1,257]{0,1,2:T(2,128)(2,1)} %slice.527), channel_id=1, source_target_pairs={{8,0},{16,8},{24,16},{9,1},{17,9},{25,17},{10,2},{18,10},{26,18},{... | collective-permute-start | bytes 74024 | tf_op jit(solution)/shard_map/ppermute | solution.py:31
  670.0 11.5 %collective-permute-start.31 = (f32[48,16,1]{0,1,2:T(8,128)S(1)}, f32[48,16,1]{0,1,2:T(8,128)S(1)}, u32[]{:S(2)}, u32[]{:S(2)}) collective-permute-start(f32[48,16,1]{0,1,2:T(8,128)S(1)} %slice.419), channel_id=1, source_target_pairs={{1,0},{2,1},{3,2},{4,3},{5,4},{6,5},{7,6},{9,8},{10,9},{11,10},{12... | collective-permute-start | bytes 9224 | tf_op jit(solution)/shard_map/ppermute | solution.py:31
  679.4 214.1 %all-gather.11.cloned.1.call-start = ((), (), s32[]{:S(2)}) async-start(), calls=%async_computation.5 | async-start | bytes 9732096 | tf_op jit(solution)/shard_map/all_gather | solution.py:114
  700.3 110.1 %collective-permute-start.32 = (bf16[48,2,256]{0,1,2:T(2,128)(2,1)S(1)}, bf16[48,2,256]{0,1,2:T(2,128)(2,1)S(1)}, u32[]{:S(2)}, u32[]{:S(2)}) collective-permute-start(bf16[48,2,256]{0,1,2:T(2,128)(2,1)S(1)} %get-tuple-element.122), channel_id=1, source_target_pairs={{0,8},{8,16},{16,24},{1,9},{9,17},{17,25},{2,10},{10,18},{18,26},{... | collective-permute-start | bytes 147464 | tf_op jit(solution)/shard_map/ppermute | solution.py:20
  704.4 106.1 %collective-permute-start.33 = (bf16[48,2,256]{0,1,2:T(2,128)(2,1)S(1)}, bf16[48,2,256]{0,1,2:T(2,128)(2,1)S(1)}, u32[]{:S(2)}, u32[]{:S(2)}) collective-permute-start(bf16[48,2,256]{0,1,2:T(2,128)(2,1)S(1)} %get-tuple-element.123), channel_id=1, source_target_pairs={{8,0},{16,8},{24,16},{9,1},{17,9},{25,17},{10,2},{18,10},{26,18},{... | collective-permute-start | bytes 147464 | tf_op jit(solution)/shard_map/ppermute | solution.py:23
  810.8 14.4 %collective-permute-start.34 = (bf16[48,20,2]{2,0,1:T(8,128)(2,1)S(1)}, bf16[48,20,2]{2,0,1:T(8,128)(2,1)S(1)}, u32[]{:S(2)}, u32[]{:S(2)}) collective-permute-start(bf16[48,20,2]{2,0,1:T(8,128)(2,1)S(1)} %get-tuple-element.152), channel_id=1, source_target_pairs={{0,1},{1,2},{2,3},{3,4},{4,5},{5,6},{6,7},{8,9},{9,10},{10,11},{11... | collective-permute-start | bytes 11528 | tf_op jit(solution)/shard_map/ppermute | solution.py:20
  814.2 12.5 %collective-permute-start.35 = (bf16[48,20,2]{2,0,1:T(8,128)(2,1)S(1)}, bf16[48,20,2]{2,0,1:T(8,128)(2,1)S(1)}, u32[]{:S(2)}, u32[]{:S(2)}) collective-permute-start(bf16[48,20,2]{2,0,1:T(8,128)(2,1)S(1)} %get-tuple-element.153), channel_id=1, source_target_pairs={{1,0},{2,1},{3,2},{4,3},{5,4},{6,5},{7,6},{9,8},{10,9},{11,10},{12... | collective-permute-start | bytes 11528 | tf_op jit(solution)/shard_map/ppermute | solution.py:23
  (81 other events, 1027.3 us)
Sparse Core Ops, SparseCore 0:
  109.0 130.0 all-reduce.3
  242.0 81.0 all-gather.6
  394.4 130.1 all-reduce.5
  527.3 81.0 all-gather.8
  679.5 128.4 all-reduce.7
  810.8 82.6 all-gather.10
